TPU v7x, 32 devices: a whole 2x2x4 slice. The times are simulated.
32 devices in a mesh: ctx: 8 (over z, y), fsdp: 4 (over x, core).
Axes of the slice: x: 2, y: 2, z: 4, core: 2. Of those that a mesh axis runs over, the one named last changes fastest.
Arguments:
- tokens: bfloat16 [8192, 1024], P(('fsdp', 'ctx')), may hold values from -6 to 6
- cotangent: bfloat16 [8192, 1024], P(('fsdp', 'ctx')), may hold values from -6 to 6
- gain_attn: bfloat16 [1024], P('fsdp'), may hold values from 0.5 to 1.5
- w_qkv: bfloat16 [1024, 3072], P('fsdp'), may hold values from -0.25 to 0.25
- w_out: bfloat16 [1024, 1024], P('fsdp'), may hold values from -0.75 to 0.75
- gain_ffn: bfloat16 [1024], P('fsdp'), may hold values from 0.5 to 1.5
- w_gate_up: bfloat16 [1024, 5632], P('fsdp'), may hold values from -0.1875 to 0.1875
- w_down: bfloat16 [2816, 1024], P('fsdp'), may hold values from -0.109375 to 0.109375
- lengths: int32 [4, 4], P('fsdp'), may hold values from 1 to 1024, 2048 in all within a row
- block_order: int32 [4, 32], P('fsdp'), may hold values from 0 to 31, each once within a row
Outputs:
- output: bfloat16 [8192, 1024], P(('fsdp', 'ctx'))
- grad_tokens: bfloat16 [8192, 1024], P(('fsdp', 'ctx'))
- grad_gain_attn: float32 [1024], P('fsdp')
- grad_w_qkv: float32 [1024, 3072], P('fsdp')
- grad_w_out: float32 [1024, 1024], P('fsdp')
- grad_gain_ffn: float32 [1024], P('fsdp')
- grad_w_gate_up: float32 [1024, 5632], P('fsdp')
- grad_w_down: float32 [2816, 1024], P('fsdp')
Inputs may be any that keep to these rules, and one draw needn't show every extreme that they name: Each row gives the lengths of the 4 sequences that fill one group's 2048 tokens, in sequence order; the longest is exactly 1024. `block_order`: each row is a permutation of the 32 blocks of one group.
All inputs are finite; a program needn't handle non-finite values.
Results may differ from a plain program's by a relative error of at most 0.024.
Values may be sent and summed in bfloat16 or wider, within the bound.
No kernel may reach another device: no remote copies, remote signals or barrier semaphores. Data moves between devices by JAX's collectives and lax.ppermute only.
A program may use at most 256 MiB of HBM per device.

v0:
```python
import math
import jax
import jax.numpy as jnp
from jax import lax
from jax.sharding import PartitionSpec as P

HEADS = 16
EPS = 1e-05
MASKED = -1e30


def contract_rows(left, right):
    return lax.dot_general(
        left, right, (((0,), (0,)), ((), ())), preferred_element_type=jnp.float32
    )


def against_rows(left, right):
    return lax.dot_general(
        left, right, (((1,), (1,)), ((), ())), preferred_element_type=jnp.float32
    )


def rms_forward(rows):
    inverse = lax.rsqrt(jnp.mean(rows * rows, axis=1, keepdims=True) + EPS)
    return (rows * inverse, inverse)


def rms_backward(normed, inverse, gain, grad_out):
    scaled = grad_out * gain
    inner = jnp.mean(scaled * normed, axis=1, keepdims=True)
    return (inverse * (scaled - normed * inner), jnp.sum(grad_out * normed, axis=0))


def visible(pos_query, seg_query, pos_keys, seg_keys):
    return (seg_query[:, None] == seg_keys[None, :]) & (pos_keys[None, :] <= pos_query[:, None])


def key_block(kv_all, pos_all, seg_all, start, block_rows, heads, depth):
    width = heads * depth
    kv_block = lax.dynamic_slice_in_dim(kv_all, start, block_rows, 0)
    key_heads = kv_block[:, :width].reshape(block_rows, heads, depth)
    value_heads = kv_block[:, width:].reshape(block_rows, heads, depth)
    pos_block = lax.dynamic_slice_in_dim(pos_all, start, block_rows, 0)
    seg_block = lax.dynamic_slice_in_dim(seg_all, start, block_rows, 0)
    return (key_heads, value_heads, pos_block, seg_block)


def attend_forward(query_heads, kv_all, pos_query, seg_query, pos_all, seg_all, scale):
    rows, heads, depth = query_heads.shape
    total_keys = kv_all.shape[0]
    block_rows = min(512, total_keys)

    def one_step(carry, number):
        run_max, run_sum, accum = carry
        key_heads, value_heads, pos_block, seg_block = key_block(
            kv_all, pos_all, seg_all, number * block_rows, block_rows, heads, depth
        )
        allowed = visible(pos_query, seg_query, pos_block, seg_block)[:, None, :]
        scores = (
            jnp.einsum("qhd,khd->qhk", query_heads, key_heads, preferred_element_type=jnp.float32)
            * scale
        )
        scores = jnp.where(allowed, scores, MASKED)
        new_max = jnp.maximum(run_max, jnp.max(scores, axis=2))
        expo = jnp.where(allowed, jnp.exp(scores - new_max[:, :, None]), 0.0)
        factor = jnp.exp(run_max - new_max)
        run_sum = run_sum * factor + jnp.sum(expo, axis=2)
        accum = accum * factor[:, :, None] + jnp.einsum(
            "qhk,khd->qhd",
            expo.astype(jnp.bfloat16),
            value_heads,
            preferred_element_type=jnp.float32,
        )
        return ((new_max, run_sum, accum), None)

    start_state = (
        jnp.full((rows, heads), MASKED, jnp.float32),
        jnp.zeros((rows, heads), jnp.float32),
        jnp.zeros((rows, heads, depth), jnp.float32),
    )
    final_state, unused = lax.scan(
        one_step, start_state, jnp.arange(total_keys // block_rows, dtype=jnp.int32)
    )
    run_max, run_sum, accum = final_state
    return (accum / run_sum[:, :, None], run_max + jnp.log(run_sum))


def attend_backward(
    query_heads, kv_all, grad_heads, delta, log_total, pos_query, seg_query, pos_all, seg_all, scale
):
    rows, heads, depth = query_heads.shape
    width = heads * depth
    total_keys = kv_all.shape[0]
    block_rows = min(512, total_keys)

    def one_step(grad_query, number):
        key_heads, value_heads, pos_block, seg_block = key_block(
            kv_all, pos_all, seg_all, number * block_rows, block_rows, heads, depth
        )
        allowed = visible(pos_query, seg_query, pos_block, seg_block)[:, None, :]
        scores = (
            jnp.einsum("qhd,khd->qhk", query_heads, key_heads, preferred_element_type=jnp.float32)
            * scale
        )
        probs = jnp.where(allowed, jnp.exp(scores - log_total[:, :, None]), 0.0)
        dprob = jnp.einsum(
            "qhd,khd->qhk", grad_heads, value_heads, preferred_element_type=jnp.float32
        )
        grad_scores = (probs * (dprob - delta[:, :, None])).astype(jnp.bfloat16)
        grad_query = grad_query + jnp.einsum(
            "qhk,khd->qhd", grad_scores, key_heads, preferred_element_type=jnp.float32
        )
        grad_keys = (
            jnp.einsum("qhk,qhd->khd", grad_scores, query_heads, preferred_element_type=jnp.float32)
            * scale
        )
        grad_values = jnp.einsum(
            "qhk,qhd->khd",
            probs.astype(jnp.bfloat16),
            grad_heads,
            preferred_element_type=jnp.float32,
        )
        return (
            grad_query,
            jnp.concatenate(
                [grad_keys.reshape(block_rows, width), grad_values.reshape(block_rows, width)],
                axis=1,
            ),
        )

    grad_query, grad_pairs = lax.scan(
        one_step,
        jnp.zeros((rows, heads, depth), jnp.float32),
        jnp.arange(total_keys // block_rows, dtype=jnp.int32),
    )
    return (grad_query * scale, grad_pairs.reshape(total_keys, 2 * width))


def body(
    tokens, cotangent, gain_attn, w_qkv, w_out, gain_ffn, w_gate_up, w_down, lengths, block_order
):
    rows, width = tokens.shape
    heads = HEADS
    depth = width // heads
    scale = depth ** (-0.5)
    ctx_count = lax.axis_size("ctx")
    fsdp_count = lax.axis_size("fsdp")
    group_rows = rows * ctx_count
    factor = 1.0 / math.sqrt(rows * ctx_count * fsdp_count)
    gathered = (
        lax.all_gather(gain_attn, "fsdp", axis=0, tiled=True),
        lax.all_gather(w_qkv, "fsdp", axis=0, tiled=True),
        lax.all_gather(w_out, "fsdp", axis=0, tiled=True),
        lax.all_gather(gain_ffn, "fsdp", axis=0, tiled=True),
        lax.all_gather(w_gate_up, "fsdp", axis=0, tiled=True),
        lax.all_gather(w_down, "fsdp", axis=0, tiled=True),
    )
    gain_one, weight_qkv, weight_out, gain_two, weight_gu, weight_down = gathered
    gain_one = gain_one.astype(jnp.float32)
    gain_two = gain_two.astype(jnp.float32)
    hidden_width = weight_down.shape[0]
    block_size = group_rows // block_order.shape[1]
    pos_all = (
        block_order[0][:, None] * block_size + jnp.arange(block_size, dtype=jnp.int32)[None, :]
    ).reshape(group_rows)
    ends = jnp.cumsum(lengths[0])
    seg_all = jnp.sum((pos_all[:, None] >= ends[None, :]).astype(jnp.int32), axis=1)
    offset = lax.axis_index("ctx") * rows
    pos_query = lax.dynamic_slice_in_dim(pos_all, offset, rows, 0)
    seg_query = lax.dynamic_slice_in_dim(seg_all, offset, rows, 0)
    inputs = tokens.astype(jnp.float32)
    normed_one, inverse_one = rms_forward(inputs)
    attn_in = (normed_one * gain_one).astype(jnp.bfloat16)
    qkv = jnp.dot(attn_in, weight_qkv, preferred_element_type=jnp.float32).astype(jnp.bfloat16)
    query_flat = qkv[:, :width]
    query_heads = query_flat.reshape(rows, heads, depth)
    key_value = qkv[:, width:]
    kv_all = lax.all_gather(key_value, "ctx", axis=0, tiled=True)
    out_heads, log_total = attend_forward(
        query_heads, kv_all, pos_query, seg_query, pos_all, seg_all, scale
    )
    attn_low = out_heads.reshape(rows, width).astype(jnp.bfloat16)
    resid = inputs + jnp.dot(attn_low, weight_out, preferred_element_type=jnp.float32)
    normed_two, inverse_two = rms_forward(resid)
    ffn_in = (normed_two * gain_two).astype(jnp.bfloat16)
    gate_up = jnp.dot(ffn_in, weight_gu, preferred_element_type=jnp.float32)
    gate = gate_up[:, :hidden_width]
    upward = gate_up[:, hidden_width:]
    sigma = jax.nn.sigmoid(gate)
    active = gate * sigma
    hidden = (active * upward).astype(jnp.bfloat16)
    output = (resid + jnp.dot(hidden, weight_down, preferred_element_type=jnp.float32)).astype(
        jnp.bfloat16
    )
    grad_hidden = against_rows(cotangent, weight_down)
    grad_gate = grad_hidden * upward * (sigma + gate * sigma * (1.0 - sigma))
    grad_up = grad_hidden * active
    grad_gu = jnp.concatenate([grad_gate, grad_up], axis=1).astype(jnp.bfloat16)
    grad_ffn_in = against_rows(grad_gu, weight_gu)
    grad_norm_two, grad_gain_two = rms_backward(normed_two, inverse_two, gain_two, grad_ffn_in)
    grad_resid = cotangent.astype(jnp.float32) + grad_norm_two
    grad_branch = grad_resid.astype(jnp.bfloat16)
    grad_attn = against_rows(grad_branch, weight_out).astype(jnp.bfloat16)
    grad_heads = grad_attn.reshape(rows, heads, depth)
    delta = jnp.sum(grad_heads.astype(jnp.float32) * out_heads, axis=2)
    kv_back = lax.all_gather(key_value, "ctx", axis=0, tiled=True)
    grad_query, grad_pair_terms = attend_backward(
        query_heads,
        kv_back,
        grad_heads,
        delta,
        log_total,
        pos_query,
        seg_query,
        pos_all,
        seg_all,
        scale,
    )
    grad_pairs = lax.psum_scatter(
        grad_pair_terms.astype(jnp.bfloat16), "ctx", scatter_dimension=0, tiled=True
    )
    grad_qkv = jnp.concatenate(
        [grad_query.reshape(rows, width).astype(jnp.bfloat16), grad_pairs], axis=1
    )
    grad_attn_in = against_rows(grad_qkv, weight_qkv)
    grad_norm_one, grad_gain_one = rms_backward(normed_one, inverse_one, gain_one, grad_attn_in)
    grad_tokens = (grad_resid + grad_norm_one).astype(jnp.bfloat16)
    terms = (
        grad_gain_one,
        contract_rows(attn_in, grad_qkv),
        contract_rows(attn_low, grad_branch),
        grad_gain_two,
        contract_rows(ffn_in, grad_gu),
        contract_rows(hidden, cotangent),
    )
    partial_shards = (
        lax.psum_scatter(
            terms[0].astype(jnp.bfloat16), "fsdp", scatter_dimension=0, tiled=True
        ).astype(jnp.float32),
        lax.psum_scatter(
            terms[1].astype(jnp.bfloat16), "fsdp", scatter_dimension=0, tiled=True
        ).astype(jnp.float32),
        lax.psum_scatter(
            terms[2].astype(jnp.bfloat16), "fsdp", scatter_dimension=0, tiled=True
        ).astype(jnp.float32),
        lax.psum_scatter(
            terms[3].astype(jnp.bfloat16), "fsdp", scatter_dimension=0, tiled=True
        ).astype(jnp.float32),
        lax.psum_scatter(
            terms[4].astype(jnp.bfloat16), "fsdp", scatter_dimension=0, tiled=True
        ).astype(jnp.float32),
        lax.psum_scatter(
            terms[5].astype(jnp.bfloat16), "fsdp", scatter_dimension=0, tiled=True
        ).astype(jnp.float32),
    )
    shards = (
        lax.psum(partial_shards[0].astype(jnp.bfloat16), "ctx").astype(jnp.float32),
        lax.psum(partial_shards[1].astype(jnp.bfloat16), "ctx").astype(jnp.float32),
        lax.psum(partial_shards[2].astype(jnp.bfloat16), "ctx").astype(jnp.float32),
        lax.psum(partial_shards[3].astype(jnp.bfloat16), "ctx").astype(jnp.float32),
        lax.psum(partial_shards[4].astype(jnp.bfloat16), "ctx").astype(jnp.float32),
        lax.psum(partial_shards[5].astype(jnp.bfloat16), "ctx").astype(jnp.float32),
    )
    return (
        output,
        grad_tokens,
        shards[0] * factor,
        shards[1] * factor,
        shards[2] * factor,
        shards[3] * factor,
        shards[4] * factor,
        shards[5] * factor,
    )


def solution(mesh):
    in_specs = (
        P(("fsdp", "ctx"), None),
        P(("fsdp", "ctx"), None),
        P("fsdp"),
        P("fsdp", None),
        P("fsdp", None),
        P("fsdp"),
        P("fsdp", None),
        P("fsdp", None),
        P("fsdp", None),
        P("fsdp", None),
    )
    out_specs = (
        P(("fsdp", "ctx"), None),
        P(("fsdp", "ctx"), None),
        P("fsdp"),
        P("fsdp", None),
        P("fsdp", None),
        P("fsdp"),
        P("fsdp", None),
        P("fsdp", None),
    )
    return jax.shard_map(body, mesh=mesh, in_specs=in_specs, out_specs=out_specs, check_vma=False)
```

profile of v0, /device:TPU:0, one launch (start us, length us, event | category | flops | bytes accessed | tf_op | source)
XLA Modules:
  0.0 1096.1 jit_solution(1279736065175315214)
XLA Ops:
  8.6 6.0 all-gather
  15.8 42.8 %all-gather.8.cloned.1.call-done = bf16[1024,3072]{1,0:T(8,128)(2,1)} async-done(((bf16[256,3072]{1,0:T(8,128)(2,1)}), bf16[1024,3072]{1,0:T(8,128)(2,1)}) %all-gather.8.cloned.1.call-update) | async-done | bytes 6291472 | tf_op jit(solution)/shard_map/all_gather | solution.py:153
  72.8 117.0 %all-gather.10.cloned.1.call-done = bf16[2048,2048]{1,0:T(8,128)(2,1)} async-done(((bf16[256,2048]{1,0:T(8,128)(2,1)}), bf16[2048,2048]{1,0:T(8,128)(2,1)}) %all-gather.10.cloned.1.call-update) | async-done | bytes 8388624 | tf_op jit(solution)/shard_map/all_gather | solution.py:179
  189.8 12.4 %copy.64 = bf16[2048,2048]{0,1:T(8,128)(2,1)} copy(bf16[2048,2048]{1,0:T(8,128)(2,1)} %all-gather.10.cloned.1.call-done) | data formatting | bytes 16777216
  202.1 73.7 %while.28 = (s32[]{:T(128)}, f32[256,16]{0,1:T(8,128)S(1)}, f32[256,16]{0,1:T(8,128)S(1)}, f32[256,16,64]{0,2,1:T(8,128)}, s32[256]{0:T(256)S(1)}, /*index=5*/s3...) while((s32[]{:T(128)}, f32[256,16]{0,1:T(8,128)S(1)}, ...), condition=%wide.region_6.7_spmd.clone, body=%wide.region_3.6_spmd.clone.sunk | while | flops 565334016 | bytes 68434200 | solution.py:82
  222.9 6.1 fusion.113
  279.8 9.9 all-gather.14.cloned.1.call-done
  289.7 9.4 fusion.54
  299.1 35.4 %all-gather.16.cloned.1.call-done = bf16[2816,1024]{1,0:T(8,128)(2,1)} async-done(((bf16[704,1024]{1,0:T(8,128)(2,1)}), bf16[2816,1024]{1,0:T(8,128)(2,1)}) %all-gather.16.cloned.1.call-update) | async-done | bytes 5767184 | tf_op jit(solution)/shard_map/all_gather | solution.py:157
  334.6 8.8 multiply_convert_fusion.1
  343.4 7.5 multiply_reduce_fusion
  356.2 102.9 %while.29 = (s32[]{:T(128)}, f32[256,16,64]{0,2,1:T(8,128)}, bf16[4,512,2048]{2,1,0:T(8,128)(2,1)}, s32[4]{0:T(128)S(1)}, bf16[2048,2048]{0,1:T(8,128)(2,1)}, /*...) while((s32[]{:T(128)}, f32[256,16,64]{0,2,1:T(8,128)}, ...), condition=%wide.region_11.12_spmd.clone, body=%wide.region_10.11_spmd.clone.sunk | while | flops 1369309184 | bytes 118946184 | solution.py:132
  462.5 5.6 convolution_convert_fusion.1
  469.4 7.9 convolution_convert_fusion
  480.8 127.4 %reduce-scatter.6.cloned.1.call-done = bf16[256,2048]{1,0:T(8,128)(2,1)} async-done(((bf16[2048,2048]{1,0:T(8,128)(2,1)}), bf16[256,2048]{1,0:T(8,128)(2,1)}) %reduce-scatter.6.cloned.1.call-update) | async-done | bytes 1048592 | tf_op jit(solution)/shard_map/reduce_scatter | solution.py:220
  608.2 5.8 convolution_convert_fusion.2
  614.1 27.8 %reduce-scatter.10.cloned.1.call-done = bf16[256,1024]{1,0:T(8,128)(2,1)} async-done(((bf16[1024,1024]{1,0:T(8,128)(2,1)}), bf16[256,1024]{1,0:T(8,128)(2,1)}) %reduce-scatter.10.cloned.1.call-update) | async-done | bytes 524304 | tf_op jit(solution)/shard_map/reduce_scatter | solution.py:244
  641.9 58.0 %reduce-scatter.14.cloned.1.call-done = bf16[704,1024]{1,0:T(8,128)(2,1)} async-done(((bf16[2816,1024]{1,0:T(8,128)(2,1)}), bf16[704,1024]{1,0:T(8,128)(2,1)}) %reduce-scatter.14.cloned.1.call-update) | async-done | bytes 1441808 | tf_op jit(solution)/shard_map/reduce_scatter | solution.py:253
  699.9 95.0 %reduce-scatter.12.cloned.1.call-done = bf16[256,5632]{1,0:T(8,128)(2,1)} async-done(((bf16[1024,5632]{1,0:T(8,128)(2,1)}), bf16[256,5632]{1,0:T(8,128)(2,1)}) %reduce-scatter.12.cloned.1.call-update) | async-done | bytes 2883600 | tf_op jit(solution)/shard_map/reduce_scatter | solution.py:250
  794.9 61.0 %reduce-scatter.8.cloned.1.call-done = bf16[256,3072]{1,0:T(8,128)(2,1)} async-done(((bf16[1024,3072]{1,0:T(8,128)(2,1)}), bf16[256,3072]{1,0:T(8,128)(2,1)}) %reduce-scatter.8.cloned.1.call-update) | async-done | bytes 1572880 | tf_op jit(solution)/shard_map/reduce_scatter | solution.py:241
  857.1 5.6 fusion.35
  867.6 6.1 all-reduce.4
  873.8 22.6 %all-reduce.2 = (bf16[256]{0:T(256)(128)(2,1)S(1)}, bf16[256]{0:T(256)(128)(2,1)S(1)}) all-reduce(bf16[256]{0:T(256)(128)(2,1)S(1)} %dynamic-slice.1, bf16[256]{0:T(256)(128)(2,1)S(1)} %dynamic-slice.3), channel_id=1, replica_groups=mesh['ctx'=8,'fsdp'=4] {'ctx'}, use_global_device_ids=true, to_apply=%region_16.17 | all-reduce | flops 512 | bytes 2048 | tf_op jit(solution)/shard_map/psum | solution.py:258
  898.1 181.6 %all-reduce.7.cloned.1.call-done = (bf16[256,3072]{1,0:T(8,128)(2,1)}, bf16[256,1024]{1,0:T(8,128)(2,1)}, bf16[256,5632]{1,0:T(8,128)(2,1)}, bf16[704,1024]{1,0:T(8,128)(2,1)}) async-done(((bf16[256,3072]{1,0:T(8,128)(2,1)}, bf16[256,1024]{1,0:T(8,128)(2,1)}, bf16[256,5632]{1,0:T(8,128)(2,1)}, bf16[704,1024]{1,0:T(8,128)(2,1)}), (bf16[256,3072]{1,0:T(8,128)(2,1)}, bf16[256,1024]{1,0:T(8,128)(2,1)}, ...) | async-done | bytes 6422544 | tf_op jit(solution)/shard_map/psum | solution.py:259
  (258 shorter events, 215.8 us)
Async XLA Ops:
  7.2 51.5 %all-gather.8.cloned.1.call-start = ((), (), s32[]{:S(2)}) async-start(), calls=%async_computation.5 | async-start | bytes 7864320 | tf_op jit(solution)/shard_map/all_gather | solution.py:153
  7.9 181.9 %all-gather.10.cloned.1.call-start = ((), (), s32[]{:S(2)}) async-start(), calls=%async_computation.6 | async-start | bytes 9437184 | tf_op jit(solution)/shard_map/all_gather | solution.py:179
  14.6 48.9 %copy-start.23 = (f32[4,1,256]{2,1,0:T(1,128)}, f32[4,1,256]{2,1,0:T(1,128)S(1)}, u32[]{:S(2)}) copy-start(f32[4,1,256]{2,1,0:T(1,128)S(1)} %convert_element_type.150) | copy-start | bytes 12292
  15.8 47.7 %copy-start.25 = (f32[256]{0:T(256)}, f32[256]{0:T(256)S(1)}, u32[]{:S(2)}) copy-start(f32[256]{0:T(256)S(1)} %add_rsqrt_fusion.1) | copy-start | bytes 3076
  64.7 212.5 %all-gather.12.cloned.1.call-start = ((), (), s32[]{:S(2)}) async-start(), calls=%async_computation.7 | async-start | bytes 2621440 | tf_op jit(solution)/shard_map/all_gather | solution.py:154
  65.4 224.3 %all-gather.14.cloned.1.call-start = ((), (), s32[]{:S(2)}) async-start(), calls=%async_computation.8 | async-start | bytes 14417920 | tf_op jit(solution)/shard_map/all_gather | solution.py:156
  66.0 268.6 %all-gather.16.cloned.1.call-start = ((), (), s32[]{:S(2)}) async-start(), calls=%async_computation.9 | async-start | bytes 7208960 | tf_op jit(solution)/shard_map/all_gather | solution.py:157
  66.6 541.7 %reduce-scatter.6.cloned.1.call-start = ((), (), s32[]{:S(2)}) async-start(), calls=%async_computation.10 | async-start | bytes 9437184 | tf_op jit(solution)/shard_map/reduce_scatter | solution.py:220
  202.1 75.1 %copy-start.8 = (bf16[256,1024]{1,0:T(8,128)(2,1)S(1)}, bf16[256,1024]{1,0:T(8,128)(2,1)}, u32[]{:S(2)}) copy-start(bf16[256,1024]{1,0:T(8,128)(2,1)} %param.14) | copy-start | bytes 1572868
  277.2 22.0 %copy-start.9 = (bf16[256,16,64]{0,2,1:T(8,128)(2,1)}, bf16[256,16,64]{0,2,1:T(8,128)(2,1)S(1)}, u32[]{:S(2)}) copy-start(bf16[256,16,64]{0,2,1:T(8,128)(2,1)S(1)} %fusion.45) | copy-start | bytes 1572868
  279.8 71.2 %copy-start.3 = (f32[256,1024]{1,0:T(8,128)}, f32[256,1024]{1,0:T(8,128)S(1)}, u32[]{:S(2)}) copy-start(f32[256,1024]{1,0:T(8,128)S(1)} %get-tuple-element.410) | copy-start | bytes 3145732
  289.7 44.9 %copy-start.15 = (bf16[256,1024]{1,0:T(8,128)(2,1)S(1)}, bf16[256,1024]{1,0:T(8,128)(2,1)}, u32[]{:S(2)}) copy-start(bf16[256,1024]{1,0:T(8,128)(2,1)} %param.15) | copy-start | bytes 1572868
  343.4 7.6 copy-start.19
  343.4 7.6 copy-start.20
  343.4 7.6 copy-start.16
  343.4 7.9 copy-start.7
  459.1 182.8 %reduce-scatter.10.cloned.1.call-start = ((), (), s32[]{:S(2)}) async-start(), calls=%async_computation.12 | async-start | bytes 2621440 | tf_op jit(solution)/shard_map/reduce_scatter | solution.py:244
  462.5 237.5 %reduce-scatter.14.cloned.1.call-start = ((), (), s32[]{:S(2)}) async-start(), calls=%async_computation.14 | async-start | bytes 7208960 | tf_op jit(solution)/shard_map/reduce_scatter | solution.py:253
  468.2 326.7 %reduce-scatter.12.cloned.1.call-start = ((), (), s32[]{:S(2)}) async-start(), calls=%async_computation.13 | async-start | bytes 14417920 | tf_op jit(solution)/shard_map/reduce_scatter | solution.py:250
  477.3 130.9 %copy-start.24 = (f32[4,1,256]{2,1,0:T(1,128)S(1)}, f32[4,1,256]{2,1,0:T(1,128)}, u32[]{:S(2)}) copy-start(f32[4,1,256]{2,1,0:T(1,128)} %copy-done.23) | copy-start | bytes 12292
  477.3 130.9 %copy-start.26 = (f32[256]{0:T(256)S(1)}, f32[256]{0:T(256)}, u32[]{:S(2)}) copy-start(f32[256]{0:T(256)} %copy-done.25) | copy-start | bytes 3076
  477.3 378.5 %reduce-scatter.8.cloned.1.call-start = ((), (), s32[]{:S(2)}) async-start(), calls=%async_computation.11 | async-start | bytes 7864320 | tf_op jit(solution)/shard_map/reduce_scatter | solution.py:241
  614.1 241.8 %copy-start.30 = (u32[32]{0:T(128)S(1)}, u32[32]{0:T(128)}, u32[]{:S(2)}) copy-start(u32[32]{0:T(128)} %constant.83) | copy-start | bytes 388
  614.1 465.5 %all-reduce.7.cloned.1.call-start = ((), (), s32[]{:S(2)}) async-start(), calls=%async_computation.15 | async-start | bytes 12845056 | tf_op jit(solution)/shard_map/psum | solution.py:259
  (33 other events, 130.0 us)
Sparse Core Ops, SparseCore 0:
  9.6 49.0 all-gather.7
  64.8 124.9 all-gather.9
  191.3 20.7 all-gather.11
  213.5 76.1 all-gather.13
  291.1 43.3 all-gather.15
  459.2 148.9 reduce-scatter.5
  611.5 30.4 reduce-scatter.9
  645.0 54.8 reduce-scatter.13
  702.7 92.1 reduce-scatter.11
  797.5 58.3 reduce-scatter.7
  860.5 219.0 all-reduce.6
where the time goes:
time: 1100 us
  waiting for transfers between devices  758 us (69%)
  matrix products  169 us (15%)
  local copies, waits for them, and re-layouts  63.6 us (6%)
  other arithmetic  44.1 us (4%)
  blocking collectives  39.9 us (4%)
  between operations  14.9 us (1%)
    psum x1, waiting for transfers between devices, body(): lax.psum(partial_shards[1].astype(jnp.bfloat16), 'ctx').astype(jnp.float32)  182 us
    reduce_scatter x1, waiting for transfers between devices, body(): lax.psum_scatter(grad_pair_terms.astype(jnp.bfloat16), 'ctx', scatter_dim...  127 us
    all_gather x1, waiting for transfers between devices, body(): kv_all = lax.all_gather(key_value, 'ctx', axis=0, tiled=True)  117 us
    reduce_scatter x1, waiting for transfers between devices, body(): lax.psum_scatter(terms[4].astype(jnp.bfloat16), 'fsdp', scatter_dimension...  95 us
    reduce_scatter x1, waiting for transfers between devices, body(): lax.psum_scatter(terms[1].astype(jnp.bfloat16), 'fsdp', scatter_dimension...  61 us
    reduce_scatter x1, waiting for transfers between devices, body(): lax.psum_scatter(terms[5].astype(jnp.bfloat16), 'fsdp', scatter_dimension...  58 us
    all_gather x1, waiting for transfers between devices, body(): lax.all_gather(w_qkv, 'fsdp', axis=0, tiled=True)  42.8 us
    all_gather x1, waiting for transfers between devices, body(): lax.all_gather(w_down, 'fsdp', axis=0, tiled=True)  35.4 us
  transfers between devices with their start and end apart: 11, of which 10 were waited for; matrix products, arithmetic and copies ran while one was open for 12% of the time, Pallas kernels for 0%

commit v1 on v0

--- a/solution.py
+++ b/solution.py
@@ -7,6 +7,11 @@
 HEADS = 16
 EPS = 1e-05
 MASKED = -1e30
+
+
+def gather_and_add(x, name):
+    parts = lax.all_gather(x, name)
+    return jnp.sum(parts, axis=0)
 
 
 def contract_rows(left, right):
@@ -256,7 +261,7 @@
     )
     shards = (
         lax.psum(partial_shards[0].astype(jnp.bfloat16), "ctx").astype(jnp.float32),
-        lax.psum(partial_shards[1].astype(jnp.bfloat16), "ctx").astype(jnp.float32),
+        gather_and_add(partial_shards[1].astype(jnp.bfloat16), "ctx").astype(jnp.float32),
         lax.psum(partial_shards[2].astype(jnp.bfloat16), "ctx").astype(jnp.float32),
         lax.psum(partial_shards[3].astype(jnp.bfloat16), "ctx").astype(jnp.float32),
         lax.psum(partial_shards[4].astype(jnp.bfloat16), "ctx").astype(jnp.float32),

time: 1100 us -> 1230 us (1.12)
  waiting for transfers between devices: 758 us -> 882 us
    all_gather x0 -> x1, waiting for transfers between devices: none -> 169 us  [gather_and_add(): parts = lax.all_gather(x, name)]
    psum x1, waiting for transfers between devices: 182 us -> 137 us  [body(): lax.psum(partial_shards[2].astype(jnp.bfloat16), 'ctx').astype(jnp.float32)]
  transfers between devices with their start and end apart: 11 -> 12, of which waited for: 10 -> 11; matrix products, arithmetic and copies ran while one was open for 12% -> 11% of each run, Pallas kernels for 0% -> 0%
where the time goes in v1:
time: 1230 us
  waiting for transfers between devices  882 us (72%)
  matrix products  170 us (14%)
  local copies, waits for them, and re-layouts  63.7 us (5%)
  other arithmetic  52.3 us (4%)
  blocking collectives  39.5 us (3%)
  between operations  15.4 us (1%)
    all_gather x1, waiting for transfers between devices, gather_and_add(): parts = lax.all_gather(x, name)  169 us
    psum x1, waiting for transfers between devices, body(): lax.psum(partial_shards[2].astype(jnp.bfloat16), 'ctx').astype(jnp.float32)  137 us
    reduce_scatter x1, waiting for transfers between devices, body(): lax.psum_scatter(grad_pair_terms.astype(jnp.bfloat16), 'ctx', scatter_dim...  127 us
    all_gather x1, waiting for transfers between devices, body(): kv_all = lax.all_gather(key_value, 'ctx', axis=0, tiled=True)  117 us
    reduce_scatter x1, waiting for transfers between devices, body(): lax.psum_scatter(terms[4].astype(jnp.bfloat16), 'fsdp', scatter_dimension...  95 us
    reduce_scatter x1, waiting for transfers between devices, body(): lax.psum_scatter(terms[1].astype(jnp.bfloat16), 'fsdp', scatter_dimension...  60.9 us
    reduce_scatter x1, waiting for transfers between devices, body(): lax.psum_scatter(terms[5].astype(jnp.bfloat16), 'fsdp', scatter_dimension...  58 us
    all_gather x1, waiting for transfers between devices, body(): lax.all_gather(w_qkv, 'fsdp', axis=0, tiled=True)  42.8 us
  transfers between devices with their start and end apart: 12, of which 11 were waited for; matrix products, arithmetic and copies ran while one was open for 11% of the time, Pallas kernels for 0%

profile of v1, /device:TPU:0, one launch (start us, length us, event | category | flops | bytes accessed | tf_op | source)
XLA Modules:
  0.0 1228.8 jit_solution(15004018017837106554)
XLA Ops:
  8.6 6.0 all-gather.1
  15.8 42.8 %all-gather.10.cloned.1.call-done = bf16[1024,3072]{1,0:T(8,128)(2,1)} async-done(((bf16[256,3072]{1,0:T(8,128)(2,1)}), bf16[1024,3072]{1,0:T(8,128)(2,1)}) %all-gather.10.cloned.1.call-update) | async-done | bytes 6291472 | tf_op jit(solution)/shard_map/all_gather | solution.py:158
  72.8 116.9 %all-gather.12.cloned.1.call-done = bf16[2048,2048]{1,0:T(8,128)(2,1)} async-done(((bf16[256,2048]{1,0:T(8,128)(2,1)}), bf16[2048,2048]{1,0:T(8,128)(2,1)}) %all-gather.12.cloned.1.call-update) | async-done | bytes 8388624 | tf_op jit(solution)/shard_map/all_gather | solution.py:184
  189.8 12.4 %copy.64 = bf16[2048,2048]{0,1:T(8,128)(2,1)} copy(bf16[2048,2048]{1,0:T(8,128)(2,1)} %all-gather.12.cloned.1.call-done) | data formatting | bytes 16777216
  202.1 73.7 %while.28 = (s32[]{:T(128)}, f32[256,16]{0,1:T(8,128)S(1)}, f32[256,16]{0,1:T(8,128)S(1)}, f32[256,16,64]{0,2,1:T(8,128)}, s32[256]{0:T(256)S(1)}, /*index=5*/s3...) while((s32[]{:T(128)}, f32[256,16]{0,1:T(8,128)S(1)}, ...), condition=%wide.region_6.7_spmd.clone, body=%wide.region_3.6_spmd.clone.sunk | while | flops 565334016 | bytes 68434200 | solution.py:87
  222.9 6.1 fusion.113
  279.8 9.9 all-gather.16.cloned.1.call-done
  289.7 9.4 fusion.54
  299.1 35.4 %all-gather.18.cloned.1.call-done = bf16[2816,1024]{1,0:T(8,128)(2,1)} async-done(((bf16[704,1024]{1,0:T(8,128)(2,1)}), bf16[2816,1024]{1,0:T(8,128)(2,1)}) %all-gather.18.cloned.1.call-update) | async-done | bytes 5767184 | tf_op jit(solution)/shard_map/all_gather | solution.py:162
  334.6 8.8 multiply_convert_fusion.1
  343.4 7.8 multiply_reduce_fusion
  356.4 102.9 %while.29 = (s32[]{:T(128)}, f32[256,16,64]{0,2,1:T(8,128)}, bf16[4,512,2048]{2,1,0:T(8,128)(2,1)}, s32[4]{0:T(128)S(1)}, bf16[2048,2048]{0,1:T(8,128)(2,1)}, /*...) while((s32[]{:T(128)}, f32[256,16,64]{0,2,1:T(8,128)}, ...), condition=%wide.region_11.12_spmd.clone, body=%wide.region_10.11_spmd.clone.sunk | while | flops 1369309184 | bytes 118946184 | solution.py:137
  469.6 8.1 convolution_convert_fusion
  481.2 127.3 %reduce-scatter.6.cloned.1.call-done = bf16[256,2048]{1,0:T(8,128)(2,1)} async-done(((bf16[2048,2048]{1,0:T(8,128)(2,1)}), bf16[256,2048]{1,0:T(8,128)(2,1)}) %reduce-scatter.6.cloned.1.call-update) | async-done | bytes 1048592 | tf_op jit(solution)/shard_map/reduce_scatter | solution.py:225
  608.5 5.8 convolution_convert_fusion.2
  614.4 27.8 %reduce-scatter.10.cloned.1.call-done = bf16[256,1024]{1,0:T(8,128)(2,1)} async-done(((bf16[1024,1024]{1,0:T(8,128)(2,1)}), bf16[256,1024]{1,0:T(8,128)(2,1)}) %reduce-scatter.10.cloned.1.call-update) | async-done | bytes 524304 | tf_op jit(solution)/shard_map/reduce_scatter | solution.py:249
  642.2 58.0 %reduce-scatter.14.cloned.1.call-done = bf16[704,1024]{1,0:T(8,128)(2,1)} async-done(((bf16[2816,1024]{1,0:T(8,128)(2,1)}), bf16[704,1024]{1,0:T(8,128)(2,1)}) %reduce-scatter.14.cloned.1.call-update) | async-done | bytes 1441808 | tf_op jit(solution)/shard_map/reduce_scatter | solution.py:258
  700.2 95.0 %reduce-scatter.12.cloned.1.call-done = bf16[256,5632]{1,0:T(8,128)(2,1)} async-done(((bf16[1024,5632]{1,0:T(8,128)(2,1)}), bf16[256,5632]{1,0:T(8,128)(2,1)}) %reduce-scatter.12.cloned.1.call-update) | async-done | bytes 2883600 | tf_op jit(solution)/shard_map/reduce_scatter | solution.py:255
  795.3 60.9 %reduce-scatter.8.cloned.1.call-done = bf16[256,3072]{1,0:T(8,128)(2,1)} async-done(((bf16[1024,3072]{1,0:T(8,128)(2,1)}), bf16[256,3072]{1,0:T(8,128)(2,1)}) %reduce-scatter.8.cloned.1.call-update) | async-done | bytes 1572880 | tf_op jit(solution)/shard_map/reduce_scatter | solution.py:246
  868.1 6.1 all-reduce.4
  874.3 22.2 %all-reduce.2 = (bf16[256]{0:T(256)(128)(2,1)S(1)}, bf16[256]{0:T(256)(128)(2,1)S(1)}) all-reduce(bf16[256]{0:T(256)(128)(2,1)S(1)} %dynamic-slice.1, bf16[256]{0:T(256)(128)(2,1)S(1)} %dynamic-slice.3), channel_id=1, replica_groups=mesh['ctx'=8,'fsdp'=4] {'ctx'}, use_global_device_ids=true, to_apply=%region_16.17 | all-reduce | flops 512 | bytes 2048 | tf_op jit(solution)/shard_map/psum | solution.py:263
  898.2 136.6 %all-reduce.7.cloned.1.call-done = (bf16[256,1024]{1,0:T(8,128)(2,1)}, bf16[256,5632]{1,0:T(8,128)(2,1)}, bf16[704,1024]{1,0:T(8,128)(2,1)}) async-done(((bf16[256,1024]{1,0:T(8,128)(2,1)}, bf16[256,5632]{1,0:T(8,128)(2,1)}, bf16[704,1024]{1,0:T(8,128)(2,1)}), (bf16[256,1024]{1,0:T(8,128)(2,1)}, bf16[256,5632]{1,0:T(8,128)(2,1)}, bf16[704,1024]{1,0:T(8,128)(2,1)})) %all-reduce.7.cloned.1.call-update) | async-done | bytes 4849680 | tf_op jit(solution)/shard_map/psum | solution.py:265
  1043.7 168.8 %all-gather.20.cloned.1.call-done = bf16[2048,3072]{1,0:T(8,128)(2,1)} async-done(((bf16[256,3072]{1,0:T(8,128)(2,1)}), bf16[2048,3072]{1,0:T(8,128)(2,1)}) %all-gather.20.cloned.1.call-update) | async-done | bytes 12582928 | tf_op jit(solution)/shard_map/all_gather | solution.py:13
  1212.5 7.3 reduce_sum.100
  (258 shorter events, 228.3 us)
Async XLA Ops:
  7.2 51.5 %all-gather.10.cloned.1.call-start = ((), (), s32[]{:S(2)}) async-start(), calls=%async_computation.5 | async-start | bytes 7864320 | tf_op jit(solution)/shard_map/all_gather | solution.py:158
  7.9 181.9 %all-gather.12.cloned.1.call-start = ((), (), s32[]{:S(2)}) async-start(), calls=%async_computation.6 | async-start | bytes 9437184 | tf_op jit(solution)/shard_map/all_gather | solution.py:184
  14.6 48.9 %copy-start.21 = (f32[4,1,256]{2,1,0:T(1,128)}, f32[4,1,256]{2,1,0:T(1,128)S(1)}, u32[]{:S(2)}) copy-start(f32[4,1,256]{2,1,0:T(1,128)S(1)} %convert_element_type.152) | copy-start | bytes 12292
  15.8 47.7 %copy-start.23 = (f32[256]{0:T(256)}, f32[256]{0:T(256)S(1)}, u32[]{:S(2)}) copy-start(f32[256]{0:T(256)S(1)} %add_rsqrt_fusion.1) | copy-start | bytes 3076
  64.7 212.5 %all-gather.14.cloned.1.call-start = ((), (), s32[]{:S(2)}) async-start(), calls=%async_computation.7 | async-start | bytes 2621440 | tf_op jit(solution)/shard_map/all_gather | solution.py:159
  65.4 224.3 %all-gather.16.cloned.1.call-start = ((), (), s32[]{:S(2)}) async-start(), calls=%async_computation.8 | async-start | bytes 14417920 | tf_op jit(solution)/shard_map/all_gather | solution.py:161
  66.0 268.6 %all-gather.18.cloned.1.call-start = ((), (), s32[]{:S(2)}) async-start(), calls=%async_computation.9 | async-start | bytes 7208960 | tf_op jit(solution)/shard_map/all_gather | solution.py:162
  66.6 541.9 %reduce-scatter.6.cloned.1.call-start = ((), (), s32[]{:S(2)}) async-start(), calls=%async_computation.10 | async-start | bytes 9437184 | tf_op jit(solution)/shard_map/reduce_scatter | solution.py:225
  202.1 75.1 %copy-start.8 = (bf16[256,1024]{1,0:T(8,128)(2,1)S(1)}, bf16[256,1024]{1,0:T(8,128)(2,1)}, u32[]{:S(2)}) copy-start(bf16[256,1024]{1,0:T(8,128)(2,1)} %param.14) | copy-start | bytes 1572868
  277.1 22.0 %copy-start.9 = (bf16[256,16,64]{0,2,1:T(8,128)(2,1)}, bf16[256,16,64]{0,2,1:T(8,128)(2,1)S(1)}, u32[]{:S(2)}) copy-start(bf16[256,16,64]{0,2,1:T(8,128)(2,1)S(1)} %fusion.45) | copy-start | bytes 1572868
  279.8 71.5 %copy-start.3 = (f32[256,1024]{1,0:T(8,128)}, f32[256,1024]{1,0:T(8,128)S(1)}, u32[]{:S(2)}) copy-start(f32[256,1024]{1,0:T(8,128)S(1)} %get-tuple-element.409) | copy-start | bytes 3145732
  289.7 44.9 %copy-start.15 = (bf16[256,1024]{1,0:T(8,128)(2,1)S(1)}, bf16[256,1024]{1,0:T(8,128)(2,1)}, u32[]{:S(2)}) copy-start(bf16[256,1024]{1,0:T(8,128)(2,1)} %param.15) | copy-start | bytes 1572868
  343.4 7.8 copy-start.19
  343.4 7.9 copy-start.16
  343.4 8.2 copy-start.7
  459.3 182.9 %reduce-scatter.10.cloned.1.call-start = ((), (), s32[]{:S(2)}) async-start(), calls=%async_computation.12 | async-start | bytes 2621440 | tf_op jit(solution)/shard_map/reduce_scatter | solution.py:249
  462.7 237.5 %reduce-scatter.14.cloned.1.call-start = ((), (), s32[]{:S(2)}) async-start(), calls=%async_computation.14 | async-start | bytes 7208960 | tf_op jit(solution)/shard_map/reduce_scatter | solution.py:258
  468.4 326.8 %reduce-scatter.12.cloned.1.call-start = ((), (), s32[]{:S(2)}) async-start(), calls=%async_computation.13 | async-start | bytes 14417920 | tf_op jit(solution)/shard_map/reduce_scatter | solution.py:255
  477.8 130.7 %copy-start.22 = (f32[4,1,256]{2,1,0:T(1,128)S(1)}, f32[4,1,256]{2,1,0:T(1,128)}, u32[]{:S(2)}) copy-start(f32[4,1,256]{2,1,0:T(1,128)} %copy-done.21) | copy-start | bytes 12292
  477.8 130.7 %copy-start.24 = (f32[256]{0:T(256)S(1)}, f32[256]{0:T(256)}, u32[]{:S(2)}) copy-start(f32[256]{0:T(256)} %copy-done.23) | copy-start | bytes 3076
  477.8 378.4 %reduce-scatter.8.cloned.1.call-start = ((), (), s32[]{:S(2)}) async-start(), calls=%async_computation.11 | async-start | bytes 7864320 | tf_op jit(solution)/shard_map/reduce_scatter | solution.py:246
  614.3 241.9 %copy-start.28 = (u32[32]{0:T(128)S(1)}, u32[32]{0:T(128)}, u32[]{:S(2)}) copy-start(u32[32]{0:T(128)} %constant.85) | copy-start | bytes 388
  614.4 420.4 %all-reduce.7.cloned.1.call-start = ((), (), s32[]{:S(2)}) async-start(), calls=%async_computation.16 | async-start | bytes 9699328 | tf_op jit(solution)/shard_map/psum | solution.py:265
  795.3 417.2 %all-gather.20.cloned.1.call-start = ((), (), s32[]{:S(2)}) async-start(), calls=%async_computation.15 | async-start | bytes 14155776 | tf_op jit(solution)/shard_map/all_gather | solution.py:13
  (32 other events, 131.9 us)
Sparse Core Ops, SparseCore 0:
  9.6 49.0 all-gather.9
  64.8 124.9 all-gather.11
  191.3 20.7 all-gather.13
  213.5 76.1 all-gather.15
  291.1 43.3 all-gather.17
  459.5 148.9 reduce-scatter.5
  611.8 30.4 reduce-scatter.9
  645.3 54.8 reduce-scatter.13
  703.0 92.2 reduce-scatter.11
  797.8 58.3 reduce-scatter.7
  860.2 174.5 all-reduce.6
  1037.1 175.3 all-gather.19
